TPU v7x, 32 devices: a whole 2x2x4 slice. The times are simulated.
32 devices in a mesh: row: 8 (over y, x, core), col: 4 (over z).
Axes of the slice: x: 2, y: 2, z: 4, core: 2. Of those that a mesh axis runs over, the one named last changes fastest.
Arguments:
- chol: float32 [12288, 640], P(('row', 'col')), may hold values from -6 to 6
- eps_occ: float32 [48], replicated, may hold values from -2 to -0.5
- eps_vir: float32 [256], replicated, may hold values from 0.3 to 3
Outputs:
- work: float32 [12288, 640], P(('row', 'col'))
- energies: float32 [2], replicated
All inputs are finite; a program needn't handle non-finite values.
Results may differ from a plain program's by a relative error of at most 0.00013.
Values sent between devices are 32-bit elements; how exact they have to be, the bound alone decides.
A program may use at most 192 MiB of HBM per device.

v0:
```python
import jax
import jax.numpy as jnp
from jax import lax
from jax.sharding import PartitionSpec as P

ITERS = 2


def shards(chol, eps_occ, eps_vir):
    n_row = lax.axis_size("row")
    n_col = lax.axis_size("col")
    row_index = lax.axis_index("row")
    col_index = lax.axis_index("col")
    shard = chol.shape[0]
    width = chol.shape[1]
    occupied = eps_occ.shape[0]
    virtual = eps_vir.shape[0]
    shard_virtuals = shard // occupied
    block_virtuals = n_col * shard_virtuals
    total = virtual * occupied
    row_vir = lax.dynamic_slice_in_dim(eps_vir, row_index * block_virtuals, block_virtuals, 0)
    row_pair = row_vir[:, None] - eps_occ[None, :]
    col_vir = lax.dynamic_slice_in_dim(
        eps_vir.reshape(n_row, block_virtuals), col_index * shard_virtuals, shard_virtuals, 1
    ).reshape(n_row * shard_virtuals)
    col_pair = col_vir[:, None] - eps_occ[None, :]
    chol_cols = lax.all_gather(
        chol.reshape(shard_virtuals, occupied, width), "row", axis=0, tiled=True
    )
    work = jnp.zeros_like(chol)
    sums = []
    for step in range(ITERS):
        factor = chol + work
        rows_factor = lax.all_gather(factor, "col", axis=0, tiled=True)
        piece = lax.all_gather(
            factor.reshape(shard_virtuals, occupied, width), "row", axis=0, tiled=True
        )
        count = piece.shape[0]
        product = lax.dot_general(
            rows_factor,
            piece.reshape(count * occupied, width),
            (((1,), (1,)), ((), ())),
            precision=lax.Precision.HIGHEST,
            preferred_element_type=jnp.float32,
        )
        direct = product.reshape(block_virtuals, occupied, count, occupied)
        numerator = 2.0 * direct - jnp.transpose(direct, (0, 3, 2, 1))
        denominator = row_pair[:, :, None, None] + col_pair[None, None, :, :]
        tile = (-numerator / (jnp.float32(total) * denominator)).reshape(
            block_virtuals * occupied, count * occupied
        )
        chol_piece = chol_cols.reshape(count * occupied, width)
        partial_value = jnp.dot(
            tile, chol_piece, precision=lax.Precision.HIGHEST, preferred_element_type=jnp.float32
        )
        work = lax.psum_scatter(partial_value, "col", scatter_dimension=0, tiled=True)
        local_sum = jnp.sum(chol * work)
        sums.append(local_sum)
    energies = lax.psum(jnp.stack(sums), ("row", "col"))
    return (work, energies / jnp.float32(total))


def solution(mesh):
    placed = (P(("row", "col"), None), P(), P())
    return jax.shard_map(
        shards,
        mesh=mesh,
        in_specs=placed,
        out_specs=(P(("row", "col"), None), P()),
        check_vma=False,
    )
```

profile of v0, /device:TPU:0, one launch (start us, length us, event | category | flops | bytes accessed | tf_op | source)
XLA Modules:
  0.0 1033.4 jit_solution(1675369494210483209)
XLA Ops:
  7.9 2.5 copy.8
  13.6 75.1 %all-gather.5.cloned.1.call-done = f32[1536,640]{1,0:T(8,128)} async-done(((f32[384,640]{1,0:T(8,128)}), f32[1536,640]{1,0:T(8,128)}) %all-gather.5.cloned.1.call-update) | async-done | bytes 3932176 | tf_op jit(solution)/shard_map/all_gather | solution.py:34
  88.7 53.0 %all-gather.7.cloned.1.call-done = f32[64,48,640]{2,0,1:T(8,128)} async-done(((f32[8,48,640]{2,0,1:T(8,128)}), f32[64,48,640]{2,0,1:T(8,128)}) %all-gather.7.cloned.1.call-update) | async-done | bytes 7864336 | tf_op jit(solution)/shard_map/all_gather | solution.py:35
  141.7 94.6 %fusion.6 = f32[32,48,64,48]{2,1,3,0:T(8,128)} fusion(f32[32,48,640,1]{2,1,3,0:T(8,128)} %bitcast.47, f32[64,48,640]{2,0,1:T(8,128)} %all-gather.7.cloned.1.call-done), kind=kOutput, calls=%fused_computation.11 | convolution fusion | flops 36238786560 | bytes 30670848 | tf_op jit(solution)/shard_map/dot_general | solution.py:39
  236.3 38.2 %fusion.3 = f32[32,48,64,48]{2,3,1,0:T(8,128)} fusion(f32[32,48,64,48]{2,1,3,0:T(8,128)} %fusion.6, f32[64,48]{0,1:T(8,128)S(1)} %broadcast_subtract_fusion, f32[32,48]{1,0:T(8,128)S(1)} %broadcast_subtract_fusion.1), kind=kLoop, calls=%fused_computation.5 | loop fusion | flops 28311552 | bytes 37767168 | tf_op jit(solution)/shard_map/div | solution.py:49
  274.5 43.4 %copy.10 = f32[32,48,64,48]{3,2,1,0:T(8,128)} copy(f32[32,48,64,48]{2,3,1,0:T(8,128)} %fusion.3) | data formatting | bytes 37748736 | tf_op jit(solution)/shard_map/div | solution.py:49
  317.9 47.0 %reshape.91 = f32[1536,3072]{1,0:T(8,128)} reshape(f32[32,48,64,48]{3,2,1,0:T(8,128)} %copy.10) | data formatting | bytes 37748736 | tf_op jit(solution)/shard_map/reshape | solution.py:49
  364.9 7.8 copy.11
  372.7 3.0 copy-done.1
  375.7 54.5 %fusion.8 = f32[1536,640]{1,0:T(8,128)} fusion(f32[1536,3072]{1,0:T(8,128)} %reshape.91, f32[3072,640]{1,0:T(8,128)S(1)} %bitcast.45), kind=kOutput, calls=%fused_computation.20 | convolution fusion | flops 36238786560 | bytes 30670848 | tf_op jit(solution)/shard_map/dot_general | solution.py:53
  430.2 72.7 %reduce-scatter.3.cloned.1.call-done = f32[384,640]{1,0:T(8,128)} async-done(((f32[1536,640]{1,0:T(8,128)}), f32[384,640]{1,0:T(8,128)}) %reduce-scatter.3.cloned.1.call-update) | async-done | bytes 983056 | tf_op jit(solution)/shard_map/reduce_scatter | solution.py:56
  503.0 2.2 add.40
  505.3 2.5 copy.12
  507.8 74.4 %all-gather.9.cloned.1.call-done = f32[1536,640]{1,0:T(8,128)} async-done(((f32[384,640]{1,0:T(8,128)}), f32[1536,640]{1,0:T(8,128)}) %all-gather.9.cloned.1.call-update) | async-done | bytes 3932176 | tf_op jit(solution)/shard_map/all_gather | solution.py:34
  582.2 52.2 %all-gather.11.cloned.1.call-done = f32[64,48,640]{2,0,1:T(8,128)} async-done(((f32[8,48,640]{2,0,1:T(8,128)}), f32[64,48,640]{2,0,1:T(8,128)}) %all-gather.11.cloned.1.call-update) | async-done | bytes 7864336 | tf_op jit(solution)/shard_map/all_gather | solution.py:35
  634.5 94.6 %fusion.4 = f32[32,48,64,48]{2,1,3,0:T(8,128)} fusion(f32[32,48,640,1]{2,1,3,0:T(8,128)} %bitcast.48, f32[64,48,640]{2,0,1:T(8,128)} %all-gather.11.cloned.1.call-done), kind=kOutput, calls=%fused_computation.9 | convolution fusion | flops 36238786560 | bytes 30670848 | tf_op jit(solution)/shard_map/dot_general | solution.py:39
  729.1 38.2 %fusion.1 = f32[32,48,64,48]{2,3,1,0:T(8,128)} fusion(f32[32,48,64,48]{2,1,3,0:T(8,128)} %fusion.4, f32[64,48]{0,1:T(8,128)S(1)} %broadcast_subtract_fusion, f32[32,48]{1,0:T(8,128)S(1)} %broadcast_subtract_fusion.1), kind=kLoop, calls=%fused_computation.2 | loop fusion | flops 28311552 | bytes 37767168 | tf_op jit(solution)/shard_map/div | solution.py:49
  767.3 43.4 %copy.14 = f32[32,48,64,48]{3,2,1,0:T(8,128)} copy(f32[32,48,64,48]{2,3,1,0:T(8,128)} %fusion.1) | data formatting | bytes 37748736 | tf_op jit(solution)/shard_map/div | solution.py:49
  810.7 47.0 %reshape.94 = f32[1536,3072]{1,0:T(8,128)} reshape(f32[32,48,64,48]{3,2,1,0:T(8,128)} %copy.14) | data formatting | bytes 37748736 | tf_op jit(solution)/shard_map/reshape | solution.py:49
  857.7 51.2 %fusion.9 = f32[1536,640]{1,0:T(8,128)} fusion(f32[1536,3072]{1,0:T(8,128)} %reshape.94, f32[3072,640]{1,0:T(8,128)} %bitcast.46), kind=kOutput, calls=%fused_computation.21 | convolution fusion | flops 36238786560 | bytes 30670848 | tf_op jit(solution)/shard_map/dot_general | solution.py:53
  908.9 72.8 %reduce-scatter.5.cloned.1.call-done = f32[384,640]{1,0:T(8,128)} async-done(((f32[1536,640]{1,0:T(8,128)}), f32[384,640]{1,0:T(8,128)}) %reduce-scatter.5.cloned.1.call-update) | async-done | bytes 983056 | tf_op jit(solution)/shard_map/reduce_scatter | solution.py:56
  981.7 2.1 multiply_reduce_fusion.1
  983.8 1.3 pad_maximum_fusion
  985.0 40.6 %psum.7 = f32[2]{0:T(128)S(1)} all-reduce(f32[2]{0:T(128)S(1)} %pad_maximum_fusion), channel_id=1, replica_groups=mesh['row'=8,'col'=4] {'row','col'}, use_global_device_ids=true, to_apply=%region_4.0 | all-reduce | flops 2 | bytes 16 | tf_op jit(solution)/shard_map/psum | solution.py:59
  (24 shorter events, 4.6 us)
Async XLA Ops:
  7.2 81.6 %all-gather.5.cloned.1.call-start = ((), (), s32[]{:S(2)}) async-start(), calls=%async_computation.2 | async-start | bytes 4915200 | tf_op jit(solution)/shard_map/all_gather | solution.py:34
  7.9 133.8 %all-gather.7.cloned.1.call-start = ((), (), s32[]{:S(2)}) async-start(), calls=%async_computation.3 | async-start | bytes 8847360 | tf_op jit(solution)/shard_map/all_gather | solution.py:35
  10.4 492.5 %reduce-scatter.3.cloned.1.call-start = ((), (), s32[]{:S(2)}) async-start(), calls=%async_computation.4 | async-start | bytes 4915200 | tf_op jit(solution)/shard_map/reduce_scatter | solution.py:56
  372.7 3.0 copy-start.1
  375.7 127.3 %copy-start = (f32[384,640]{1,0:T(8,128)S(1)}, f32[384,640]{1,0:T(8,128)}, u32[]{:S(2)}) copy-start(f32[384,640]{1,0:T(8,128)} %param.3) | copy-start | bytes 2949124
  430.2 152.0 %all-gather.9.cloned.1.call-start = ((), (), s32[]{:S(2)}) async-start(), calls=%async_computation.5 | async-start | bytes 4915200 | tf_op jit(solution)/shard_map/all_gather | solution.py:34
  505.2 129.3 %all-gather.11.cloned.1.call-start = ((), (), s32[]{:S(2)}) async-start(), calls=%async_computation.6 | async-start | bytes 8847360 | tf_op jit(solution)/shard_map/all_gather | solution.py:35
  507.8 473.9 %reduce-scatter.5.cloned.1.call-start = ((), (), s32[]{:S(2)}) async-start(), calls=%async_computation.7 | async-start | bytes 4915200 | tf_op jit(solution)/shard_map/reduce_scatter | solution.py:56
  857.7 124.0 %copy-start.2 = (f32[384,640]{1,0:T(8,128)S(1)}, f32[384,640]{1,0:T(8,128)}, u32[]{:S(2)}) copy-start(f32[384,640]{1,0:T(8,128)} %reduce-scatter.3.cloned.1.call-done) | copy-start | bytes 2949124
Sparse Core Ops, SparseCore 0:
  9.5 79.1 all-gather.4
  91.2 50.4 all-gather.6
  430.3 72.6 reduce-scatter.2
  505.4 76.8 all-gather.8
  584.0 50.4 all-gather.10
  909.0 72.6 reduce-scatter.4
where the time goes:
time: 1050 us; the launch traced here: 1030 us
  waiting for transfers between devices  401 us (38%)
  matrix products  295 us (28%)
  local copies, waits for them, and re-layouts  198 us (19%)
  other arithmetic  84 us (8%)
  blocking collectives  40.6 us (4%)
  between operations  14.5 us (1%)
    dot_general x2, matrix products, shards(): lax.dot_general(rows_factor, piece.reshape(count * occupied, width), (((1...  189 us
    all_gather x2, waiting for transfers between devices, shards(): rows_factor = lax.all_gather(factor, 'col', axis=0, tiled=True)  150 us
    reduce_scatter x2, waiting for transfers between devices, shards(): lax.psum_scatter(partial_value, 'col', scatter_dimension=0, tiled=True)  145 us
    dot_general x2, matrix products, shards(): jnp.dot(tile, chol_piece, precision=lax.Precision.HIGHEST, preferred_elem...  106 us
    all_gather x2, waiting for transfers between devices, shards(): lax.all_gather(factor.reshape(shard_virtuals, occupied, width), 'row', ax...  105 us
    reshape x2, local copies, waits for them, and re-layouts, shards(): (-numerator / (jnp.float32(total) * denominator)).reshape(block_virtuals...  94 us
    div x2, local copies, waits for them, and re-layouts, shards(): -numerator / (jnp.float32(total) * denominator)  86.8 us
    div x2, other arithmetic, shards(): -numerator / (jnp.float32(total) * denominator)  76.5 us
  transfers between devices with their start and end apart: 6, of which 6 were waited for; matrix products, arithmetic and copies ran while one was open for 1% of the time, Pallas kernels for 0%

commit v1 on v0

v1 whole, which is shorter than its diff:
```python
import functools

import jax
import jax.numpy as jnp
from jax import lax
from jax.experimental import pallas as pl
from jax.experimental.pallas import tpu as pltpu
from jax.sharding import PartitionSpec as P

ITERS = 2
LANES = 128
NT = (((1,), (1,)), ((), ()))


def split(x):
    high = x.astype(jnp.bfloat16)
    low = (x - high.astype(jnp.float32)).astype(jnp.bfloat16)
    return high, low


def flat(ref, index):
    pieces = [ref[part, index] for part in range(ref.shape[0])]
    return pieces[0] if len(pieces) == 1 else jnp.concatenate(pieces, axis=0)


def kernel(steps, rows_ref, cols_ref, chol_ref, rpair_ref, cpair_ref, out_ref, rows, cols, chol, direct, high_tile, low_tile):
    step = pl.program_id(0)
    parts, occupied, shard_virtuals, width = rows_ref.shape
    height = parts * shard_virtuals
    block = occupied // steps
    breadth = cols_ref.shape[0] * cols_ref.shape[2]
    span = block * breadth
    group = LANES // breadth

    @pl.when(step == 0)
    def _():
        def one(index, carry):
            high, low = split(flat(rows_ref, index))
            at = pl.ds(pl.multiple_of(index * height, height), height)
            rows[at, :width] = high
            rows[at, width:] = low
            return carry

        lax.fori_loop(0, occupied, one, 0)

    @pl.when(step < steps)
    def _():
        for index in range(block):
            high, low = split(flat(cols_ref, index))
            cols[index * breadth : (index + 1) * breadth, :width] = low
            cols[index * breadth : (index + 1) * breadth, width:] = high
            high, low = split(flat(chol_ref, index))
            at = pl.ds(pl.multiple_of(step * span + index * breadth, breadth), breadth)
            chol[at, :width] = high
            chol[at, width:] = low

        def one(index, carry):
            at = pl.ds(pl.multiple_of(index * block * height, block * height), block * height)
            value = lax.dot_general(rows[at, :], cols[...], NT, preferred_element_type=jnp.float32)
            value += lax.dot_general(rows[at, :width], cols[:, width:], NT, preferred_element_type=jnp.float32)
            direct[at, pl.ds(pl.multiple_of(step * span, span), span)] = value
            return carry

        lax.fori_loop(0, steps, one, 0)

    @pl.when(step >= steps)
    def _():
        first = (step - steps) * block
        lane = lax.broadcasted_iota(jnp.int32, (height, LANES), 1) // breadth

        def one(index, carry):
            lead = first + index * group
            columns = pl.ds(pl.multiple_of(lead * breadth, LANES), LANES)
            bottoms = [rpair_ref[lead + own] for own in range(group)]
            for other in range(occupied // group):
                swapped = [direct[pl.ds((other * group + m) * height, height), columns] for m in range(group)]
                to = slice(other * LANES, (other + 1) * LANES)
                tops = cpair_ref[other : other + 1, :]
                for own in range(group):
                    exchange = swapped[0] if own == 0 else pltpu.roll(swapped[0], (LANES - own * breadth) % LANES, 1)
                    for m in range(1, group):
                        shift = ((m - own) * breadth) % LANES
                        moved = pltpu.roll(swapped[m], shift, 1) if shift else swapped[m]
                        exchange = jnp.where(lane == m, moved, exchange)
                    at = pl.ds(pl.multiple_of((lead + own) * height, height), height)
                    value = (exchange - 2.0 * direct[at, to]) / (bottoms[own] + tops)
                    high, low = split(value)
                    put = pl.ds(pl.multiple_of((index * group + own) * height, height), height)
                    high_tile[put, to] = high
                    low_tile[put, to] = low
            return carry

        lax.fori_loop(0, block // group, one, 0)
        both = jnp.dot(high_tile[...], chol[...], preferred_element_type=jnp.float32)
        value = both[:, :width] + both[:, width:]
        value += jnp.dot(low_tile[...], chol[:, :width], preferred_element_type=jnp.float32)
        value = value.reshape(block, parts, shard_virtuals, width)
        for part in range(parts):
            out_ref[part] = value[:, part]


def update(rows, cols, chol, rpair, cpair):
    parts, occupied, shard_virtuals, width = rows.shape
    height = parts * shard_virtuals
    breadth = cols.shape[0] * cols.shape[2]
    steps = 6
    block = occupied // steps
    pair_columns = occupied * breadth
    column_block = (cols.shape[0], block, cols.shape[2], width)

    def of_columns(step):
        return (0, jnp.minimum(step, steps - 1), 0, 0)

    return pl.pallas_call(
        functools.partial(kernel, steps),
        grid=(2 * steps,),
        out_shape=jax.ShapeDtypeStruct(rows.shape, jnp.float32),
        in_specs=[
            pl.BlockSpec(rows.shape, lambda step: (0, 0, 0, 0)),
            pl.BlockSpec(column_block, of_columns),
            pl.BlockSpec(column_block, of_columns),
            pl.BlockSpec(rpair.shape, lambda step: (0, 0, 0)),
            pl.BlockSpec(cpair.shape, lambda step: (0, 0)),
        ],
        out_specs=pl.BlockSpec((parts, block, shard_virtuals, width), lambda step: (0, jnp.maximum(step - steps, 0), 0, 0)),
        scratch_shapes=[
            pltpu.VMEM((occupied * height, 2 * width), jnp.bfloat16),
            pltpu.VMEM((block * breadth, 2 * width), jnp.bfloat16),
            pltpu.VMEM((pair_columns, 2 * width), jnp.bfloat16),
            pltpu.VMEM((occupied * height, pair_columns), jnp.float32),
            pltpu.VMEM((block * height, pair_columns), jnp.bfloat16),
            pltpu.VMEM((block * height, pair_columns), jnp.bfloat16),
        ],
        compiler_params=pltpu.CompilerParams(
            dimension_semantics=("arbitrary",), vmem_limit_bytes=66 * 1000 * 1000
        ),
        cost_estimate=pl.CostEstimate(
            flops=12 * occupied * height * pair_columns * width, bytes_accessed=4 * width * (2 * occupied * height + 2 * pair_columns), transcendentals=0
        ),
    )(rows, cols, chol, rpair, cpair)


def gather(x, axis):
    parts = lax.all_gather(x, axis, axis=0)
    if x.shape[1] % 8:
        parts = jnp.transpose(parts, (1, 0, 2, 3)).reshape(1, x.shape[0], -1, x.shape[2])
    return parts


def shards(chol, eps_occ, eps_vir):
    n_row = lax.axis_size("row")
    n_col = lax.axis_size("col")
    row_index = lax.axis_index("row")
    col_index = lax.axis_index("col")
    shard, width = chol.shape
    occupied = eps_occ.shape[0]
    virtual = eps_vir.shape[0]
    shard_virtuals = shard // occupied
    block_virtuals = n_col * shard_virtuals
    total = virtual * occupied
    scale = jnp.float32(total)
    row_vir = lax.dynamic_slice_in_dim(eps_vir, row_index * block_virtuals, block_virtuals, 0)
    col_vir = lax.dynamic_slice_in_dim(
        eps_vir.reshape(n_row, block_virtuals), col_index * shard_virtuals, shard_virtuals, 1
    ).reshape(n_row * shard_virtuals)
    rpair = scale * (row_vir[None, :] - eps_occ[:, None])
    rpair = jnp.broadcast_to(rpair[:, :, None], (occupied, block_virtuals, LANES))
    cpair = (scale * (col_vir[None, :] - eps_occ[:, None])).reshape(-1, LANES)
    chol_t = jnp.transpose(chol.reshape(shard_virtuals, occupied, width), (1, 0, 2))
    chol_cols = gather(chol_t, "row")
    factor = chol_t
    sums = []
    for step in range(ITERS):
        rows = gather(factor, "col")
        cols = chol_cols if step == 0 else gather(factor, "row")
        partial_value = update(rows, cols, chol_cols, rpair, cpair)
        if shard_virtuals % 8:
            partial_value = jnp.transpose(
                partial_value.reshape(occupied, n_col, shard_virtuals, width), (1, 0, 2, 3)
            )
        work = lax.psum_scatter(partial_value, "col", scatter_dimension=0, tiled=False)
        factor = chol_t + work
        sums.append(jnp.sum(chol_t * work))
    energies = lax.psum(jnp.stack(sums), ("row", "col"))
    return jnp.transpose(work, (1, 0, 2)).reshape(shard, width), energies / scale


def solution(mesh):
    placed = (P(("row", "col"), None), P(), P())
    return jax.shard_map(
        shards,
        mesh=mesh,
        in_specs=placed,
        out_specs=(P(("row", "col"), None), P()),
        check_vma=False,
    )
```

time: 1050 us -> 603 us (0.57); the launches traced: 1030 us -> 602 us
  matrix products: 295 us -> 0 us
  local copies, waits for them, and re-layouts: 198 us -> 6.7 us
  Pallas kernels: 0 us -> 127 us
  other arithmetic: 84 us -> 7.17 us
    dot_general x4 -> x0, matrix products: 295 us -> none  [the longest x2 189 us: shards(): lax.dot_general(rows_factor, piece.reshape(count * occupied, width), (((1...]
    pallas_call x0 -> x2, Pallas kernels: none -> 127 us  [update(): pl.pallas_call(functools.partial(kernel, steps), grid=(2 * steps,), out_s...]
    reshape x4 -> x1, local copies, waits for them, and re-layouts: 98.9 us -> 2.47 us  [shards(): chol.reshape(shard_virtuals, occupied, width)]
    div x2 -> x0, local copies, waits for them, and re-layouts: 86.8 us -> none  [shards(): -numerator / (jnp.float32(total) * denominator)]
    div x3 -> x1, other arithmetic: 77 us -> 0.51 us  [shards(): energies / scale]
  transfers between devices with their start and end apart: 6 -> 6, of which waited for: 6 -> 6; matrix products, arithmetic and copies ran while one was open for 1% -> 0% of each run, Pallas kernels for 0% -> 0%
where the time goes in v1:
time: 603 us; the launch traced here: 602 us
  waiting for transfers between devices  407 us (67%)
  Pallas kernels  127 us (21%)
  blocking collectives  40.6 us (7%)
  between operations  14.2 us (2%)
  other arithmetic  7.17 us (1%)
  local copies, waits for them, and re-layouts  6.7 us (1%)
    all_gather x4, waiting for transfers between devices, gather(): parts = lax.all_gather(x, axis, axis=0)  260 us
    reduce_scatter x2, waiting for transfers between devices, shards(): lax.psum_scatter(partial_value, 'col', scatter_dimension=0, tiled=False)  145 us
    pallas_call x2, Pallas kernels, update(): pl.pallas_call(functools.partial(kernel, steps), grid=(2 * steps,), out_s...  127 us
    psum x1, blocking collectives, shards(): energies = lax.psum(jnp.stack(sums), ('row', 'col'))  40.6 us
  transfers between devices with their start and end apart: 6, of which 6 were waited for; matrix products, arithmetic and copies ran while one was open for 0% of the time, Pallas kernels for 0%

profile of v1, /device:TPU:0, one launch (start us, length us, event | category | flops | bytes accessed | tf_op | source)
XLA Modules:
  0.0 602.4 jit_solution(13390608413664488092)
XLA Ops:
  7.2 2.5 copy.16
  9.8 0.7 all-gather.11.cloned.1.call-update
  10.8 0.1 sub.44
  10.8 0.1 sub.46
  10.9 0.1 sub.48
  11.0 0.1 sub.49
  11.1 0.1 sub.50
  11.2 0.6 subtract_multiply_fusion.1.cpair_ref
  11.9 77.4 %all-gather.9.cloned.1.call-done = f32[192,8,640]{2,1,0:T(8,128)} async-done(((f32[48,8,640]{2,1,0:T(8,128)}), f32[192,8,640]{2,1,0:T(8,128)}) %all-gather.9.cloned.1.call-update) | async-done | bytes 3932176 | tf_op jit(solution)/shard_map/all_gather | solution.py:144
  89.3 53.1 %all-gather.11.cloned.1.call-done = f32[384,8,640]{2,1,0:T(8,128)} async-done(((f32[48,8,640]{2,1,0:T(8,128)}), f32[384,8,640]{2,1,0:T(8,128)}) %all-gather.11.cloned.1.call-update) | async-done | bytes 7864336 | tf_op jit(solution)/shard_map/all_gather | solution.py:144
  142.4 1.2 broadcast_in_dim.2.rpair_ref
  143.6 63.5 %shard_map.50 = f32[4,48,8,640]{3,2,1,0:T(8,128)} custom-call(f32[4,48,8,640]{3,2,1,0:T(8,128)} %bitcast.39, f32[8,48,8,640]{3,2,1,0:T(8,128)} %bitcast.35, f32[8,48,8,640]{3,2,1,0:T(8,128)} %bitcast.36, f32[48,32,128]{2,1,0:T(8,128)} %broadcast_in_dim.2.rpair_ref, f32[24,128]{1,0:T(8,128)} %subtract_multiply_fusion.1.cpair_ref), custom_call_target="tpu_custom_call" | custom-call | flops 36238786560 | bytes 23592960 | tf_op jit(solution)/shard_map/pallas_call | solution.py:114
  207.2 72.7 %reduce-scatter.3.cloned.1.call-done = f32[1,48,8,640]{3,2,1,0:T(8,128)} async-done(((f32[4,48,8,640]{3,2,1,0:T(8,128)}), f32[1,48,8,640]{3,2,1,0:T(8,128)}) %reduce-scatter.3.cloned.1.call-update) | async-done | bytes 983056 | tf_op jit(solution)/shard_map/reduce_scatter | solution.py:181
  279.9 2.5 bitcast_add_fusion
  282.5 0.5 all-gather.15.cloned.1.call-update
  283.1 76.4 %all-gather.13.cloned.1.call-done = f32[192,8,640]{2,1,0:T(8,128)} async-done(((f32[48,8,640]{2,1,0:T(8,128)}), f32[192,8,640]{2,1,0:T(8,128)}) %all-gather.13.cloned.1.call-update) | async-done | bytes 3932176 | tf_op jit(solution)/shard_map/all_gather | solution.py:144
  359.4 52.9 %all-gather.15.cloned.1.call-done = f32[384,8,640]{2,1,0:T(8,128)} async-done(((f32[48,8,640]{2,1,0:T(8,128)}), f32[384,8,640]{2,1,0:T(8,128)}) %all-gather.15.cloned.1.call-update) | async-done | bytes 7864336 | tf_op jit(solution)/shard_map/all_gather | solution.py:144
  412.3 63.5 %shard_map.51 = f32[4,48,8,640]{3,2,1,0:T(8,128)} custom-call(f32[4,48,8,640]{3,2,1,0:T(8,128)} %bitcast.40, f32[8,48,8,640]{3,2,1,0:T(8,128)} %bitcast.38, f32[8,48,8,640]{3,2,1,0:T(8,128)} %bitcast.37, f32[48,32,128]{2,1,0:T(8,128)} %broadcast_in_dim.2.rpair_ref, f32[24,128]{1,0:T(8,128)} %subtract_multiply_fusion.1.cpair_ref), custom_call_target="tpu_custom_call" | custom-call | flops 36238786560 | bytes 23592960 | tf_op jit(solution)/shard_map/pallas_call | solution.py:114
  475.8 72.8 %reduce-scatter.5.cloned.1.call-done = f32[1,48,8,640]{3,2,1,0:T(8,128)} async-done(((f32[4,48,8,640]{3,2,1,0:T(8,128)}), f32[1,48,8,640]{3,2,1,0:T(8,128)}) %reduce-scatter.5.cloned.1.call-update) | async-done | bytes 983056 | tf_op jit(solution)/shard_map/reduce_scatter | solution.py:181
  548.6 2.1 fusion.1
  550.7 1.4 pad_maximum_fusion
  552.1 40.6 %psum.7 = f32[2]{0:T(128)S(1)} all-reduce(f32[2]{0:T(128)S(1)} %pad_maximum_fusion), channel_id=1, replica_groups=mesh['row'=8,'col'=4] {'row','col'}, use_global_device_ids=true, to_apply=%region_4.0 | all-reduce | flops 2 | bytes 16 | tf_op jit(solution)/shard_map/psum | solution.py:184
  592.7 0.5 broadcast_multiply_fusion
  593.2 2.3 copy.8
  (23 shorter events, 0.6 us)
Async XLA Ops:
  7.2 3.4 copy-start.3
  7.2 3.8 copy-start.2
  7.2 82.1 %all-gather.9.cloned.1.call-start = ((), (), s32[]{:S(2)}) async-start(), calls=%async_computation.4 | async-start | bytes 4915200 | tf_op jit(solution)/shard_map/all_gather | solution.py:144
  9.7 132.7 %all-gather.11.cloned.1.call-start = ((), (), s32[]{:S(2)}) async-start(), calls=%async_computation.5 | async-start | bytes 8847360 | tf_op jit(solution)/shard_map/all_gather | solution.py:144
  10.5 269.4 %reduce-scatter.3.cloned.1.call-start = ((), (), s32[]{:S(2)}) async-start(), calls=%async_computation.2 | async-start | bytes 4915200 | tf_op jit(solution)/shard_map/reduce_scatter | solution.py:181
  207.1 72.8 %copy-start = (f32[384,640]{1,0:T(8,128)S(1)}, f32[384,640]{1,0:T(8,128)}, u32[]{:S(2)}) copy-start(f32[384,640]{1,0:T(8,128)} %param.3) | copy-start | bytes 2949124
  207.1 152.3 %all-gather.13.cloned.1.call-start = ((), (), s32[]{:S(2)}) async-start(), calls=%async_computation.6 | async-start | bytes 4915200 | tf_op jit(solution)/shard_map/all_gather | solution.py:144
  282.4 129.9 %all-gather.15.cloned.1.call-start = ((), (), s32[]{:S(2)}) async-start(), calls=%async_computation.7 | async-start | bytes 8847360 | tf_op jit(solution)/shard_map/all_gather | solution.py:144
  283.0 265.6 %reduce-scatter.5.cloned.1.call-start = ((), (), s32[]{:S(2)}) async-start(), calls=%async_computation.3 | async-start | bytes 4915200 | tf_op jit(solution)/shard_map/reduce_scatter | solution.py:181
  475.8 72.8 %copy-start.1 = (f32[1,48,8,640]{3,2,1,0:T(8,128)S(1)}, f32[1,48,8,640]{3,2,1,0:T(8,128)}, u32[]{:S(2)}) copy-start(f32[1,48,8,640]{3,2,1,0:T(8,128)} %reduce-scatter.3.cloned.1.call-done) | copy-start | bytes 2949124
Sparse Core Ops, SparseCore 0:
  10.1 79.1 all-gather.8
  91.8 50.5 all-gather.10
  207.3 72.6 reduce-scatter.2
  282.5 76.8 all-gather.12
  361.7 50.5 all-gather.14
  476.0 72.6 reduce-scatter.4
